TPU v7x, 128 devices: a whole 4x4x4 slice. The times are simulated.
128 devices in a mesh: ctx: 8 (over x, z_hi), frame: 16 (over z_lo, y, core).
Axes of the slice: x: 4, y: 4, z: 4 (z_hi: 2, z_lo: 2; z = z_hi * 2 + z_lo), core: 2. Of those that a mesh axis runs over, the one named last changes fastest.
Arguments:
- queries: bfloat16 [4096, 4096], P('ctx', 'frame'), may hold values from -160 to 160
- keys: bfloat16 [8192, 4096], P('ctx', 'frame'), may hold values from -4 to 4
- values: bfloat16 [8192, 4096], P('ctx', 'frame'), may hold values from -6 to 6
- query_frames: int32 [256], P('ctx'), may hold values from 0 to 383, as said below
- frame_counts: int32 [512], replicated, may hold values from 0 to 16, as said below
- clip_of_frame: int32 [256], P('ctx'), may hold values from 0 to 15, as said below
- in_proj: bfloat16 [4096, 1024], P('frame'), may hold values from -0.09375 to 0.09375
- mlp_up: bfloat16 [1024, 4096], replicated, may hold values from -0.1875 to 0.1875
- mlp_down: bfloat16 [4096, 1024], replicated, may hold values from -0.09375 to 0.09375
- reward_head: float32 [1024], replicated, may hold values from -0.1875 to 0.1875
Outputs:
- query_grad: float32 [4096, 4096], P('ctx', 'frame')
- key_grad: float32 [8192, 4096], P('ctx', 'frame')
- value_grad: float32 [8192, 4096], P('ctx', 'frame')
- clip_reward: float32 [128], P(('ctx', 'frame'))
Inputs may be any that keep to these rules, and one draw needn't show every extreme that they name: `query_frames`: the query patch rows are distinct rows of the first 512 * 3 // 4 patch rows of the video, in increasing order, all of them live; the first and the last of those rows are always among them. `frame_counts`: the live tokens are a prefix of the sequence of at least three quarters of it: rows before the prefix's end are full, one row may be partly live, the rows after it have none, and the last row has none. `clip_of_frame`: within each aligned block of 32 patch row slots every clip number appears exactly 2 times.
All inputs are finite; a program needn't handle non-finite values.
Results may differ from a plain program's by a relative error of at most 0.02.
Values may be sent and summed in bfloat16 or wider, within the bound.
No kernel may reach another device: no remote copies, remote signals or barrier semaphores. Data moves between devices by JAX's collectives and lax.ppermute only.
A program may use at most 192 MiB of HBM per device.

v0:
```python
import functools
import math
import jax
import jax.numpy as jnp
from jax import lax
from jax.sharding import PartitionSpec as P

HD = 128
FTOK = 16
CLIP = 2
EPSILON = 1e-05


def rotate(values_in, position, inverse):
    row_count = values_in.shape[0]
    half_width = HD // 2
    pieces = values_in.reshape(row_count, -1, HD)
    frequency = jnp.exp(-math.log(10000.0) * jnp.arange(half_width, dtype=jnp.float32) / half_width)
    angle = position.astype(jnp.float32)[:, None] * frequency[None, :]
    cosine = jnp.cos(angle)[:, None, :]
    sine = jnp.sin(angle)[:, None, :]
    if inverse:
        sine = -sine
    first_half = pieces[:, :, :half_width]
    second_half = pieces[:, :, half_width:]
    result = jnp.concatenate(
        [first_half * cosine - second_half * sine, second_half * cosine + first_half * sine], axis=2
    )
    return result.reshape(row_count, -1)


def normalize(values_in):
    center = jnp.mean(values_in, axis=-1, keepdims=True)
    centered = values_in - center
    variance = jnp.mean(centered * centered, axis=-1, keepdims=True)
    return centered * lax.rsqrt(variance + EPSILON)


def head_scores(query_head, key_head, key_valid):
    scores = jnp.dot(query_head, key_head.T, preferred_element_type=jnp.float32) * (
        1.0 / math.sqrt(HD)
    )
    return jnp.where(key_valid[None, :], scores, -jnp.inf)


def contract_rows(left, right):
    return lax.dot_general(
        left, right, (((0,), (0,)), ((), ())), preferred_element_type=jnp.float32
    )


def score_clip(inputs, clip_live, mlp_up, mlp_down, reward_head):
    normed = normalize(inputs).astype(jnp.bfloat16)
    expanded = jax.nn.gelu(jnp.dot(normed, mlp_up, preferred_element_type=jnp.float32)).astype(
        jnp.bfloat16
    )
    hidden = jnp.dot(expanded, mlp_down, preferred_element_type=jnp.float32)
    live = clip_live.astype(jnp.float32)
    count = jnp.sum(live)
    pooled = jnp.sum(hidden * live[:, None], axis=0) / count
    return count * jnp.dot(normalize(pooled), reward_head, precision=lax.Precision.HIGHEST)


def shards(
    queries,
    keys,
    values,
    query_frames,
    frame_counts,
    clip_of_frame,
    in_proj,
    mlp_up,
    mlp_down,
    reward_head,
):
    ctx_index = lax.axis_index("ctx")
    frame_index = lax.axis_index("frame")
    query_rows = queries.shape[0]
    key_rows = keys.shape[0]
    frame_slots = query_frames.shape[0]
    width_dev = queries.shape[1]
    head_count = width_dev // HD
    key_frames = frame_counts.shape[0]
    scale = 1.0 / math.sqrt(HD)
    in_frame = jnp.arange(FTOK, dtype=jnp.int32)
    query_position = (query_frames[:, None] * FTOK + in_frame[None, :]).reshape(-1)
    key_position = ctx_index * key_rows + jnp.arange(key_rows, dtype=jnp.int32)
    key_valid = (in_frame[None, :] < frame_counts[:, None]).reshape(-1)
    frame_match = query_frames[:, None] == jnp.arange(key_frames, dtype=jnp.int32)[None, :]
    slot_counts = jnp.sum(jnp.where(frame_match, frame_counts[None, :], 0), axis=1)
    rotated_query = rotate(queries.astype(jnp.float32), query_position, False).astype(jnp.bfloat16)
    rotated_key = rotate(keys.astype(jnp.float32), key_position, False).astype(jnp.bfloat16)
    whole_key, whole_value = (
        lax.all_gather(rotated_key, "ctx", axis=0, tiled=True),
        lax.all_gather(values, "ctx", axis=0, tiled=True),
    )
    out_list, log_list, weight_list = ([], [], [])
    for head_number in range(head_count):
        lower = head_number * HD
        scores = head_scores(
            rotated_query[:, lower : lower + HD], whole_key[:, lower : lower + HD], key_valid
        )
        largest = jnp.max(scores, axis=1)
        total = jnp.sum(jnp.exp(scores - largest[:, None]), axis=1)
        log_total = largest + jnp.log(total)
        weights = jnp.exp(scores - log_total[:, None])
        out_list.append(
            jnp.dot(
                weights.astype(jnp.bfloat16),
                whole_value[:, lower : lower + HD],
                preferred_element_type=jnp.float32,
            ).astype(jnp.bfloat16)
        )
        log_list.append(log_total)
        weight_list.append(weights)
    attention_out = jnp.concatenate(out_list, axis=1)
    slot_index = jnp.arange(frame_slots, dtype=jnp.int32)
    same_clip = clip_of_frame[:, None] == clip_of_frame[None, :]
    earlier = slot_index[None, :] < slot_index[:, None]
    rank = jnp.sum(jnp.logical_and(same_clip, earlier), axis=1)
    destination = clip_of_frame * CLIP + rank
    source = jnp.sum(
        jnp.where(destination[None, :] == slot_index[:, None], slot_index[None, :], 0), axis=1
    )

    def regroup(array, order):
        framed = array.reshape(frame_slots, FTOK, array.shape[1])
        return jnp.take(framed, order, axis=0).reshape(query_rows, array.shape[1])

    grouped_out = regroup(attention_out, source)
    my_slots = lax.dynamic_slice_in_dim(source, frame_index * CLIP, CLIP)
    my_match = my_slots[:, None] == slot_index[None, :]
    my_counts = jnp.sum(jnp.where(my_match, slot_counts[None, :], 0), axis=1)
    clip_live = (in_frame[None, :] < my_counts[:, None]).reshape(-1)
    clip_inputs = lax.psum_scatter(
        jnp.dot(grouped_out, in_proj, preferred_element_type=jnp.float32),
        "frame",
        scatter_dimension=0,
        tiled=True,
    )
    scorer = functools.partial(
        score_clip, clip_live=clip_live, mlp_up=mlp_up, mlp_down=mlp_down, reward_head=reward_head
    )
    clip_value, pull_back = jax.vjp(scorer, clip_inputs)
    (input_grad,) = pull_back(jnp.ones_like(clip_value))
    low_grad = input_grad.astype(jnp.bfloat16)
    grouped_grad = jnp.dot(
        lax.all_gather(low_grad, "frame", axis=0, tiled=True),
        in_proj.T,
        preferred_element_type=jnp.float32,
    ).astype(jnp.bfloat16)
    out_grad = regroup(grouped_grad, destination)
    delta_list = []
    for head_number in range(head_count):
        lower = head_number * HD
        delta_list.append(
            jnp.sum(
                out_grad[:, lower : lower + HD].astype(jnp.float32)
                * attention_out[:, lower : lower + HD].astype(jnp.float32),
                axis=1,
            )
        )
    query_parts, grad_list, low_list = ([], [], [])
    for head_number in range(head_count):
        lower = head_number * HD
        weights = weight_list[head_number]
        weight_grad = jnp.dot(
            out_grad[:, lower : lower + HD],
            whole_value[:, lower : lower + HD].T,
            preferred_element_type=jnp.float32,
        )
        score_grad = (weights * (weight_grad - delta_list[head_number][:, None]) * scale).astype(
            jnp.bfloat16
        )
        query_parts.append(
            jnp.dot(
                score_grad, whole_key[:, lower : lower + HD], preferred_element_type=jnp.float32
            )
        )
        grad_list.append(score_grad)
        low_list.append(weights.astype(jnp.bfloat16))
    rotated_query_grad = jnp.concatenate(query_parts, axis=1)
    key_parts = []
    value_parts = []
    for head_number in range(head_count):
        lower = head_number * HD
        grad_cols = grad_list[head_number]
        weight_cols = low_list[head_number]
        key_parts.append(contract_rows(grad_cols, rotated_query[:, lower : lower + HD]))
        value_parts.append(contract_rows(weight_cols, out_grad[:, lower : lower + HD]))
    key_both = lax.psum_scatter(
        jnp.concatenate(key_parts + value_parts, axis=1), "ctx", scatter_dimension=0, tiled=True
    )
    rotated_key_grad = key_both[:, :width_dev]
    value_grad = key_both[:, width_dev:]
    query_grad = rotate(rotated_query_grad, query_position, True)
    key_grad = rotate(rotated_key_grad, key_position, True)
    return (query_grad, key_grad, value_grad, clip_value.reshape(1))


def solution(mesh):
    return jax.shard_map(
        shards,
        mesh=mesh,
        in_specs=(
            P("ctx", "frame"),
            P("ctx", "frame"),
            P("ctx", "frame"),
            P("ctx"),
            P(),
            P("ctx"),
            P("frame", None),
            P(),
            P(),
            P(),
        ),
        out_specs=(P("ctx", "frame"), P("ctx", "frame"), P("ctx", "frame"), P(("ctx", "frame"))),
        check_vma=False,
    )
```

profile of v0, /device:TPU:0, one launch (start us, length us, event | category | flops | bytes accessed | tf_op | source)
XLA Modules:
  0.0 561.1 jit_solution(8665673020066702519)
XLA Ops:
  8.6 1.8 fusion.60
  19.1 67.0 %all-gather.4.cloned.1.call-done = bf16[8192,256]{0,1:T(8,128)(2,1)} async-done(((bf16[1024,256]{0,1:T(8,128)(2,1)}), bf16[8192,256]{0,1:T(8,128)(2,1)}) %all-gather.4.cloned.1.call-update) | async-done | bytes 4194320 | tf_op jit(solution)/shard_map/all_gather | solution.py:94
  86.1 8.9 %fusion.94 = (f32[512]{0:T(512)S(1)}, f32[512,8192]{1,0:T(8,128)}) fusion(bf16[8192,256]{0,1:T(8,128)(2,1)} %all-gather.4.cloned.1.call-done, bf16[512,256]{0,1:T(8,128)(2,1)S(1)} %bitcast.41, pred[8192]{0:T(1024)(128)(4,1)S(1)} %lt.69), kind=kOutput, calls=%fused_computation.162 | convolution fusion | flops 1086324224 | bytes 19015680 | tf_op jit(solution)/shard_map/dot_general | solution.py:40
  95.0 8.7 %exponential_reduce_fusion = f32[512]{0:T(512)S(1)} fusion(f32[512,8192]{1,0:T(8,128)} %get-tuple-element.42, f32[512]{0:T(512)S(1)} %get-tuple-element.41), kind=kLoop, calls=%fused_computation.6 | loop fusion | flops 8388096 | bytes 16781312 | tf_op jit(solution)/shard_map/reduce_sum | solution.py:104
  103.7 7.2 %fusion.95 = (f32[512]{0:T(512)S(1)}, f32[512,8192]{1,0:T(8,128)}) fusion(bf16[8192,256]{0,1:T(8,128)(2,1)S(1)} %copy-done.10, bf16[512,256]{0,1:T(8,128)(2,1)S(1)} %bitcast.42, pred[8192]{0:T(1024)(128)(4,1)S(1)} %lt.69), kind=kOutput, calls=%fused_computation.163 | convolution fusion | flops 1086324224 | bytes 19015680 | tf_op jit(solution)/shard_map/dot_general | solution.py:40
  110.9 8.1 %exponential_reduce_fusion.1 = f32[512]{0:T(512)S(1)} fusion(f32[512,8192]{1,0:T(8,128)} %get-tuple-element.44, f32[512]{0:T(512)S(1)} %get-tuple-element.43), kind=kLoop, calls=%fused_computation.9 | loop fusion | flops 8388096 | bytes 16781312 | tf_op jit(solution)/shard_map/reduce_sum | solution.py:104
  119.1 10.2 %fusion.1 = bf16[512,8192]{1,0:T(8,128)(2,1)} fusion(f32[512,8192]{1,0:T(8,128)} %get-tuple-element.42, f32[512]{0:T(512)S(1)} %log_add_fusion), kind=kLoop, calls=%fused_computation.12 | loop fusion | flops 8388608 | bytes 25167872 | tf_op jit(solution)/shard_map/convert_element_type | solution.py:109
  129.3 4.0 copy-done.2
  133.3 5.0 fusion
  138.3 19.5 %all-gather.6.cloned.1.call-done = bf16[8192,256]{1,0:T(8,128)(2,1)} async-done(((bf16[1024,256]{1,0:T(8,128)(2,1)}), bf16[8192,256]{1,0:T(8,128)(2,1)}) %all-gather.6.cloned.1.call-update) | async-done | bytes 4194320 | tf_op jit(solution)/shard_map/all_gather | solution.py:95
  157.8 7.0 %fusion.18 = bf16[512,128]{0,1:T(8,128)(2,1)S(1)} fusion(bf16[512,8192]{1,0:T(8,128)(2,1)} %fusion.1, bf16[8192,256]{1,0:T(8,128)(2,1)} %all-gather.6.cloned.1.call-done), kind=kOutput, calls=%fused_computation.29 | convolution fusion | flops 1073807360 | bytes 10616832 | tf_op jit(solution)/shard_map/dot_general | solution.py:108
  164.8 4.5 fusion.15
  170.3 1.8 fusion.98
  173.4 60.6 %reduce-scatter.3.cloned.1.call-done = f32[32,1024]{1,0:T(8,128)} async-done(((f32[512,1024]{1,0:T(8,128)}), f32[32,1024]{1,0:T(8,128)}) %reduce-scatter.3.cloned.1.call-update) | async-done | bytes 131088 | tf_op jit(solution)/shard_map/reduce_scatter | solution.py:135
  236.1 5.0 fusion.61
  241.2 4.9 fusion.22
  254.5 11.0 %multiply_reduce_fusion.2 = (f32[32]{0:T(128)S(1)}, f32[32,1024]{1,0:T(8,128)S(1)}) fusion(f32[32,1024]{1,0:T(8,128)S(1)} %copy-done.9, f32[32]{0:T(128)S(1)} %broadcast_multiply_fusion, bf16[1024,4096]{1,0:T(8,128)(2,1)} %param.19, f32[32,4096]{1,0:T(8,128)S(1)} %fusion.61, bf16[4096,1024]{1,0:T(8,128)(2,1)} %param.20, f32[1024]{0:T(1024)S(1)} %add_divide_fusion, ...), kind=kOutput, calls=%fused_computation.89 | convolution fusion | flops 539820032 | bytes 17568128 | tf_op jit(solution)/shard_map/transpose(jvp())/dot_general | solution.py:54
  266.7 30.9 %all-gather.8.cloned.1.call-done = bf16[512,1024]{1,0:T(8,128)(2,1)} async-done(((bf16[32,1024]{1,0:T(8,128)(2,1)}), bf16[512,1024]{1,0:T(8,128)(2,1)}) %all-gather.8.cloned.1.call-update) | async-done | bytes 1048592 | tf_op jit(solution)/shard_map/all_gather | solution.py:148
  297.7 1.7 convolution_convert_fusion.1
  300.1 6.6 %fusion.88 = f32[8192,128]{0,1:T(8,128)} fusion(bf16[512,8192]{1,0:T(8,128)(2,1)} %fusion, bf16[512,256]{1,0:T(8,128)(2,1)S(1)} %bitcast.33), kind=kOutput, calls=%fused_computation.156 | convolution fusion | flops 1073741824 | bytes 12713984 | tf_op jit(solution)/shard_map/dot_general | solution.py:47
  306.7 6.6 %fusion.85 = f32[8192,128]{0,1:T(8,128)} fusion(bf16[512,8192]{1,0:T(8,128)(2,1)} %fusion.1, bf16[512,256]{1,0:T(8,128)(2,1)S(1)} %bitcast.34), kind=kOutput, calls=%fused_computation.153 | convolution fusion | flops 1073741824 | bytes 12713984 | tf_op jit(solution)/shard_map/dot_general | solution.py:47
  313.7 8.6 %multiply_convert_fusion = bf16[512,8192]{1,0:T(8,128)(2,1)S(1)} fusion(f32[512,8192]{1,0:T(8,128)} %get-tuple-element.42, f32[512]{0:T(512)S(1)} %multiply_reduce_fusion, f32[512]{0:T(512)S(1)} %log_add_fusion, bf16[8192,256]{1,0:T(8,128)(2,1)} %all-gather.6.cloned.1.call-done, bf16[512,256]{1,0:T(8,128)(2,1)S(1)} %bitcast.36), kind=kOutput, calls=%fused_computation.3 | convolution fusion | flops 1094713344 | bytes 27398144 | tf_op jit(solution)/shard_map/dot_general | solution.py:167
  322.3 3.3 fusion.54
  325.6 1.9 copy-done.5
  327.5 10.4 %multiply_convert_fusion.1 = bf16[512,8192]{1,0:T(8,128)(2,1)} fusion(f32[512,8192]{1,0:T(8,128)} %get-tuple-element.44, f32[512]{0:T(512)S(1)} %multiply_reduce_fusion.1, f32[512]{0:T(512)S(1)} %log_add_fusion.1, bf16[8192,256]{1,0:T(8,128)(2,1)S(1)} %copy-done.5, bf16[512,256]{1,0:T(8,128)(2,1)S(1)} %bitcast.37), kind=kOutput, calls=%fused_computation.4 | convolution fusion | flops 1094713344 | bytes 27398144 | tf_op jit(solution)/shard_map/dot_general | solution.py:167
  338.0 7.0 %fusion.57 = f32[8192,128]{0,1:T(8,128)} fusion(bf16[512,8192]{1,0:T(8,128)(2,1)} %multiply_convert_fusion.1, bf16[512,256]{0,1:T(8,128)(2,1)S(1)} %bitcast.44), kind=kOutput, calls=%fused_computation.96 | convolution fusion | flops 1073741824 | bytes 12713984 | tf_op jit(solution)/shard_map/dot_general | solution.py:47
  345.0 1.5 copy-done.8
  346.5 8.2 %pad_maximum_fusion = f32[8192,512]{0,1:T(8,128)} fusion(f32[8192,128]{0,1:T(8,128)S(1)} %copy-done.7, f32[8192,128]{0,1:T(8,128)S(1)} %copy-done.6, f32[8192,128]{0,1:T(8,128)S(1)} %copy-done.8, f32[8192,128]{0,1:T(8,128)} %fusion.57), kind=kLoop, calls=%fused_computation.2 | loop fusion | flops 12582912 | bytes 33554432 | tf_op jit(solution)/shard_map/concatenate | solution.py:192
  356.0 7.0 %fusion.6 = f32[512,128]{0,1:T(8,128)S(1)} fusion(bf16[512,8192]{1,0:T(8,128)(2,1)} %copy-done.4, bf16[8192,256]{0,1:T(8,128)(2,1)} %all-gather.4.cloned.1.call-done), kind=kOutput, calls=%fused_computation.18 | convolution fusion | flops 1073741824 | bytes 10747904 | tf_op jit(solution)/shard_map/dot_general | solution.py:176
  363.1 7.1 %fusion.12 = f32[512,128]{0,1:T(8,128)S(1)} fusion(bf16[512,8192]{1,0:T(8,128)(2,1)} %multiply_convert_fusion.1, bf16[8192,256]{0,1:T(8,128)(2,1)S(1)} %copy-done.11), kind=kOutput, calls=%fused_computation.24 | convolution fusion | flops 1073741824 | bytes 10747904 | tf_op jit(solution)/shard_map/dot_general | solution.py:176
  371.4 177.3 %reduce-scatter.5.cloned.1.call-done = f32[1024,512]{0,1:T(8,128)} async-done(((f32[8192,512]{0,1:T(8,128)}), f32[1024,512]{0,1:T(8,128)}) %reduce-scatter.5.cloned.1.call-update) | async-done | bytes 2097168 | tf_op jit(solution)/shard_map/reduce_scatter | solution.py:191
  548.6 1.7 fusion.92
  (117 shorter events, 26.5 us)
Async XLA Ops:
  7.2 163.1 %copy-start = (bf16[256,1024]{1,0:T(8,128)(2,1)S(1)}, bf16[256,1024]{1,0:T(8,128)(2,1)}, u32[]{:S(2)}) copy-start(bf16[256,1024]{1,0:T(8,128)(2,1)} %param.18) | copy-start | bytes 1572868
  7.2 78.9 %all-gather.4.cloned.1.call-start = ((), (), s32[]{:S(2)}) async-start(), calls=%async_computation.2 | async-start | bytes 4718592 | tf_op jit(solution)/shard_map/all_gather | solution.py:94
  10.3 0.7 copy-start.12
  11.9 145.9 %all-gather.6.cloned.1.call-start = ((), (), s32[]{:S(2)}) async-start(), calls=%async_computation.3 | async-start | bytes 4718592 | tf_op jit(solution)/shard_map/all_gather | solution.py:95
  12.6 221.4 %reduce-scatter.3.cloned.1.call-start = ((), (), s32[]{:S(2)}) async-start(), calls=%async_computation.4 | async-start | bytes 2228224 | tf_op jit(solution)/shard_map/reduce_scatter | solution.py:135
  14.3 0.6 copy-start.20
  14.4 0.5 copy-start.22
  95.0 8.7 %copy-start.10 = (bf16[8192,256]{0,1:T(8,128)(2,1)S(1)}, bf16[8192,256]{0,1:T(8,128)(2,1)}, u32[]{:S(2)}) copy-start(bf16[8192,256]{0,1:T(8,128)(2,1)} %all-gather.4.cloned.1.call-done) | copy-start | bytes 12582916
  119.1 14.2 %copy-start.2 = (f32[512,8192]{1,0:T(8,128)S(1)}, f32[512,8192]{1,0:T(8,128)}, u32[]{:S(2)}) copy-start(f32[512,8192]{1,0:T(8,128)} %get-tuple-element.44) | copy-start | bytes 50331652
  157.8 7.0 %copy-start.3 = (bf16[512,8192]{1,0:T(8,128)(2,1)S(1)}, bf16[512,8192]{1,0:T(8,128)(2,1)}, u32[]{:S(2)}) copy-start(bf16[512,8192]{1,0:T(8,128)(2,1)} %fusion) | copy-start | bytes 25165828
  164.8 5.3 copy-start.18
  164.8 7.3 %copy-start.23 = (s32[32]{0:T(128)S(1)}, s32[32]{0:T(128)}, u32[]{:S(2)}) copy-start(s32[32]{0:T(128)} %copy-done.22) | copy-start | bytes 388
  164.8 7.4 %copy-start.17 = (s32[512]{0:T(512)S(1)}, s32[512]{0:T(512)}, u32[]{:S(2)}) copy-start(s32[512]{0:T(512)} %param.16) | copy-start | bytes 6148
  164.8 7.4 %copy-start.19 = (s32[32]{0:T(128)S(1)}, s32[32]{0:T(128)}, u32[]{:S(2)}) copy-start(s32[32]{0:T(128)} %param.15) | copy-start | bytes 388
  172.1 125.6 %all-gather.8.cloned.1.call-start = ((), (), s32[]{:S(2)}) async-start(), calls=%async_computation.5 | async-start | bytes 1114112 | tf_op jit(solution)/shard_map/all_gather | solution.py:148
  241.2 8.9 %copy-start.16 = (f32[1024]{0:T(1024)S(1)}, f32[1024]{0:T(1024)}, u32[]{:S(2)}) copy-start(f32[1024]{0:T(1024)} %param.21) | copy-start | bytes 12292
  241.2 13.3 %copy-start.9 = (f32[32,1024]{1,0:T(8,128)S(1)}, f32[32,1024]{1,0:T(8,128)}, u32[]{:S(2)}) copy-start(f32[32,1024]{1,0:T(8,128)} %reduce-scatter.3.cloned.1.call-done) | copy-start | bytes 393220
  254.5 12.2 %copy-start.21 = (s32[32]{0:T(128)S(1)}, s32[32]{0:T(128)}, u32[]{:S(2)}) copy-start(s32[32]{0:T(128)} %copy-done.20) | copy-start | bytes 388
  266.5 282.2 %reduce-scatter.5.cloned.1.call-start = ((), (), s32[]{:S(2)}) async-start(), calls=%async_computation.6 | async-start | bytes 18874368 | tf_op jit(solution)/shard_map/reduce_scatter | solution.py:191
  322.3 15.7 %copy-start.4 = (bf16[512,8192]{1,0:T(8,128)(2,1)}, bf16[512,8192]{1,0:T(8,128)(2,1)S(1)}, u32[]{:S(2)}) copy-start(bf16[512,8192]{1,0:T(8,128)(2,1)S(1)} %multiply_convert_fusion) | copy-start | bytes 25165828
  322.3 5.2 copy-start.5
  338.0 7.1 %copy-start.6 = (f32[8192,128]{0,1:T(8,128)S(1)}, f32[8192,128]{0,1:T(8,128)}, u32[]{:S(2)}) copy-start(f32[8192,128]{0,1:T(8,128)} %fusion.88) | copy-start | bytes 12582916
  338.0 7.1 %copy-start.7 = (f32[8192,128]{0,1:T(8,128)S(1)}, f32[8192,128]{0,1:T(8,128)}, u32[]{:S(2)}) copy-start(f32[8192,128]{0,1:T(8,128)} %fusion.85) | copy-start | bytes 12582916
  338.0 8.6 %copy-start.8 = (f32[8192,128]{0,1:T(8,128)S(1)}, f32[8192,128]{0,1:T(8,128)}, u32[]{:S(2)}) copy-start(f32[8192,128]{0,1:T(8,128)} %fusion.54) | copy-start | bytes 12582916
  356.0 7.1 %copy-start.11 = (bf16[8192,256]{0,1:T(8,128)(2,1)S(1)}, bf16[8192,256]{0,1:T(8,128)(2,1)}, u32[]{:S(2)}) copy-start(bf16[8192,256]{0,1:T(8,128)(2,1)} %all-gather.4.cloned.1.call-done) | copy-start | bytes 12582916
  363.1 7.2 %copy-start.15 = (f32[512,64]{0,1:T(8,128)S(1)}, f32[512,64]{0,1:T(8,128)}, u32[]{:S(2)}) copy-start(f32[512,64]{0,1:T(8,128)} %get-tuple-element.38) | copy-start | bytes 393220
  363.1 188.6 %copy-start.13 = (f32[1024,64]{0,1:T(8,128)S(1)}, f32[1024,64]{0,1:T(8,128)}, u32[]{:S(2)}) copy-start(f32[1024,64]{0,1:T(8,128)} %copy-done.12) | copy-start | bytes 786436
  363.1 188.5 %copy-start.14 = (f32[1024,64]{0,1:T(8,128)S(1)}, f32[1024,64]{0,1:T(8,128)}, u32[]{:S(2)}) copy-start(f32[1024,64]{0,1:T(8,128)} %get-tuple-element.35) | copy-start | bytes 786436
  370.2 183.1 %copy-start.1 = (bf16[256,1024]{1,0:T(8,128)(2,1)S(1)}, bf16[256,1024]{1,0:T(8,128)(2,1)}, u32[]{:S(2)}) copy-start(bf16[256,1024]{1,0:T(8,128)(2,1)} %param.18) | copy-start | bytes 1572868
Sparse Core Ops, SparseCore 0:
  12.0 74.0 all-gather.3
  88.4 69.2 all-gather.5
  172.2 61.7 reduce-scatter.2
  266.6 31.0 all-gather.7
  354.9 193.6 reduce-scatter.4
where the time goes:
time: 570 us; the launch traced here: 561 us
  waiting for transfers between devices  356 us (62%)
  matrix products  109 us (19%)
  other arithmetic  58.8 us (10%)
  between operations  19.5 us (3%)
  local copies, waits for them, and re-layouts  17.6 us (3%)
    reduce_scatter x1, waiting for transfers between devices, shards(): lax.psum_scatter(jnp.concatenate(key_parts + value_parts, axis=1), 'ctx',...  177 us
    all_gather x1, waiting for transfers between devices, shards(): lax.all_gather(rotated_key, 'ctx', axis=0, tiled=True)  67 us
    reduce_scatter x1, waiting for transfers between devices, shards(): lax.psum_scatter(jnp.dot(grouped_out, in_proj, preferred_element_type=jnp...  60.6 us
    all_gather x1, waiting for transfers between devices, shards(): lax.all_gather(low_grad, 'frame', axis=0, tiled=True)  30.9 us
    dot_general x4, matrix products, contract_rows(): lax.dot_general(left, right, (((0,), (0,)), ((), ())), preferred_element_...  23.6 us
    all_gather x1, waiting for transfers between devices, shards(): lax.all_gather(values, 'ctx', axis=0, tiled=True)  19.5 us
    dot_general x2, matrix products, shards(): jnp.dot(out_grad[:, lower:lower + HD], whole_value[:, lower:lower + HD].T...  19.1 us
    reduce_sum x2, other arithmetic, shards(): total = jnp.sum(jnp.exp(scores - largest[:, None]), axis=1)  16.8 us
  transfers between devices with their start and end apart: 5, of which 5 were waited for; matrix products, arithmetic and copies ran while one was open for 13% of the time, Pallas kernels for 0%

commit v1 on v0

--- a/solution.py
+++ b/solution.py
@@ -9,6 +9,13 @@
 FTOK = 16
 CLIP = 2
 EPSILON = 1e-05
+
+
+def gather_over(x, name, along):
+    count = lax.axis_size(name)
+    blocks = jnp.stack([x for _ in range(count)])
+    blocks = lax.all_to_all(blocks, name, split_axis=0, concat_axis=0)
+    return jnp.concatenate(blocks, axis=along)
 
 
 def rotate(values_in, position, inverse):
@@ -91,7 +98,7 @@
     rotated_query = rotate(queries.astype(jnp.float32), query_position, False).astype(jnp.bfloat16)
     rotated_key = rotate(keys.astype(jnp.float32), key_position, False).astype(jnp.bfloat16)
     whole_key, whole_value = (
-        lax.all_gather(rotated_key, "ctx", axis=0, tiled=True),
+        gather_over(rotated_key, "ctx", 0),
         lax.all_gather(values, "ctx", axis=0, tiled=True),
     )
     out_list, log_list, weight_list = ([], [], [])

time: 570 us -> 546 us (0.958)
  waiting for transfers between devices: 356 us -> 333 us
  starting transfers between devices: 0.37 us -> 8.35 us
  other arithmetic: 58.8 us -> 52.5 us
    all_gather x1 -> x0, waiting for transfers between devices: 67 us -> none  [shards(): lax.all_gather(rotated_key, 'ctx', axis=0, tiled=True)]
    all_to_all x0 -> x1, waiting for transfers between devices: none -> 63.6 us  [gather_over(): blocks = lax.all_to_all(blocks, name, split_axis=0, concat_axis=0)]
    all_gather x1, waiting for transfers between devices: 19.5 us -> 0.02 us  [shards(): lax.all_gather(values, 'ctx', axis=0, tiled=True)]
    all_to_all x0 -> x1, starting transfers between devices: none -> 7.72 us  [gather_over(): blocks = lax.all_to_all(blocks, name, split_axis=0, concat_axis=0)]
  transfers between devices with their start and end apart: 5 -> 5, of which waited for: 5 -> 4; matrix products, arithmetic and copies ran while one was open for 13% -> 12% of each run, Pallas kernels for 0% -> 0%
where the time goes in v1:
time: 546 us; the launch traced here: 543 us
  waiting for transfers between devices  333 us (61%)
  matrix products  111 us (20%)
  other arithmetic  52.5 us (10%)
  between operations  19.6 us (4%)
  local copies, waits for them, and re-layouts  18.4 us (3%)
  starting transfers between devices  8.35 us (2%)
    reduce_scatter x1, waiting for transfers between devices, shards(): lax.psum_scatter(jnp.concatenate(key_parts + value_parts, axis=1), 'ctx',...  177 us
    all_to_all x1, waiting for transfers between devices, gather_over(): blocks = lax.all_to_all(blocks, name, split_axis=0, concat_axis=0)  63.6 us
    reduce_scatter x1, waiting for transfers between devices, shards(): lax.psum_scatter(jnp.dot(grouped_out, in_proj, preferred_element_type=jnp...  60.6 us
    all_gather x1, waiting for transfers between devices, shards(): lax.all_gather(low_grad, 'frame', axis=0, tiled=True)  30.7 us
    dot_general x4, matrix products, contract_rows(): lax.dot_general(left, right, (((0,), (0,)), ((), ())), preferred_element_...  23.5 us
    dot_general x2, matrix products, shards(): jnp.dot(out_grad[:, lower:lower + HD], whole_value[:, lower:lower + HD].T...  19.1 us
    dot_general x2, matrix products, head_scores(): jnp.dot(query_head, key_head.T, preferred_element_type=jnp.float32)  17.7 us
    reduce_sum x2, other arithmetic, shards(): total = jnp.sum(jnp.exp(scores - largest[:, None]), axis=1)  16.3 us
  transfers between devices with their start and end apart: 5, of which 4 were waited for; matrix products, arithmetic and copies ran while one was open for 12% of the time, Pallas kernels for 0%

profile of v1, /device:TPU:0, one launch (start us, length us, event | category | flops | bytes accessed | tf_op | source)
XLA Modules:
  0.0 542.8 jit_solution(8278287991324596138)
XLA Ops:
  10.0 2.2 stack.2
  12.2 7.7 %all-to-all-start = ((bf16[8,1024,256]{2,1,0:T(8,128)(2,1)}), bf16[8,1024,256]{2,1,0:T(8,128)(2,1)}, u32[]{:S(2)}, u32[]{:S(2)}) async-start(bf16[8,1024,256]{2,1,0:T(8,128)(2,1)} %stack.2), calls=%async_computation | async-start | bytes 8388608 | tf_op jit(solution)/shard_map/all_to_all | solution.py:17
  22.6 63.6 %all-to-all-done = bf16[8,1024,256]{2,1,0:T(8,128)(2,1)} async-done(((bf16[8,1024,256]{2,1,0:T(8,128)(2,1)}), bf16[8,1024,256]{2,1,0:T(8,128)(2,1)}, u32[]{:S(2)}, u32[]{:S(2)}) %all-to-all-start) | async-done | bytes 4194336 | tf_op jit(solution)/shard_map/all_to_all | solution.py:17
  86.2 9.0 %fusion.94 = (f32[512]{0:T(512)S(1)}, f32[512,8192]{1,0:T(8,128)}) fusion(bf16[8192,256]{1,0:T(8,128)(2,1)} %bitcast.2, bf16[512,256]{0,1:T(8,128)(2,1)S(1)} %bitcast.42, pred[8192]{0:T(1024)(128)(4,1)S(1)} %lt.69), kind=kOutput, calls=%fused_computation.162 | convolution fusion | flops 1086324224 | bytes 19015680 | tf_op jit(solution)/shard_map/dot_general | solution.py:47
  95.2 8.1 %exponential_reduce_fusion = f32[512]{0:T(512)S(1)} fusion(f32[512,8192]{1,0:T(8,128)} %get-tuple-element.42, f32[512]{0:T(512)S(1)} %get-tuple-element.41), kind=kLoop, calls=%fused_computation.6 | loop fusion | flops 8388096 | bytes 16781312 | tf_op jit(solution)/shard_map/reduce_sum | solution.py:111
  103.3 8.8 %fusion.95 = (f32[512]{0:T(512)S(1)}, f32[512,8192]{1,0:T(8,128)}) fusion(bf16[8192,256]{1,0:T(8,128)(2,1)} %bitcast.2, bf16[512,256]{0,1:T(8,128)(2,1)S(1)} %bitcast.43, pred[8192]{0:T(1024)(128)(4,1)S(1)} %lt.69), kind=kOutput, calls=%fused_computation.163 | convolution fusion | flops 1086324224 | bytes 19015680 | tf_op jit(solution)/shard_map/dot_general | solution.py:47
  112.1 8.2 %exponential_reduce_fusion.1 = f32[512]{0:T(512)S(1)} fusion(f32[512,8192]{1,0:T(8,128)} %get-tuple-element.44, f32[512]{0:T(512)S(1)} %get-tuple-element.43), kind=kLoop, calls=%fused_computation.9 | loop fusion | flops 8388096 | bytes 16781312 | tf_op jit(solution)/shard_map/reduce_sum | solution.py:111
  120.2 9.8 %fusion.1 = bf16[512,8192]{1,0:T(8,128)(2,1)} fusion(f32[512,8192]{1,0:T(8,128)} %get-tuple-element.42, f32[512]{0:T(512)S(1)} %log_add_fusion), kind=kLoop, calls=%fused_computation.12 | loop fusion | flops 8388608 | bytes 25167872 | tf_op jit(solution)/shard_map/convert_element_type | solution.py:116
  130.1 3.8 copy-done.2
  133.9 5.1 fusion
  139.0 7.0 %fusion.18 = bf16[512,128]{0,1:T(8,128)(2,1)S(1)} fusion(bf16[512,8192]{1,0:T(8,128)(2,1)} %fusion.1, bf16[8192,256]{1,0:T(8,128)(2,1)} %all-gather.3.cloned.1.call-done), kind=kOutput, calls=%fused_computation.29 | convolution fusion | flops 1073807360 | bytes 10616832 | tf_op jit(solution)/shard_map/dot_general | solution.py:115
  146.0 4.5 fusion.15
  151.4 1.8 fusion.98
  154.6 60.6 %reduce-scatter.3.cloned.1.call-done = f32[32,1024]{1,0:T(8,128)} async-done(((f32[512,1024]{1,0:T(8,128)}), f32[32,1024]{1,0:T(8,128)}) %reduce-scatter.3.cloned.1.call-update) | async-done | bytes 131088 | tf_op jit(solution)/shard_map/reduce_scatter | solution.py:142
  217.3 5.0 fusion.61
  222.4 4.9 fusion.22
  235.8 11.0 %multiply_reduce_fusion.2 = (f32[32]{0:T(128)S(1)}, f32[32,1024]{1,0:T(8,128)S(1)}) fusion(f32[32,1024]{1,0:T(8,128)S(1)} %copy-done.9, f32[32]{0:T(128)S(1)} %broadcast_multiply_fusion, bf16[1024,4096]{1,0:T(8,128)(2,1)} %param.19, f32[32,4096]{1,0:T(8,128)S(1)} %fusion.61, bf16[4096,1024]{1,0:T(8,128)(2,1)} %param.20, f32[1024]{0:T(1024)S(1)} %add_divide_fusion, ...), kind=kOutput, calls=%fused_computation.89 | convolution fusion | flops 539820032 | bytes 17568128 | tf_op jit(solution)/shard_map/transpose(jvp())/dot_general | solution.py:61
  248.0 30.7 %all-gather.5.cloned.1.call-done = bf16[512,1024]{1,0:T(8,128)(2,1)} async-done(((bf16[32,1024]{1,0:T(8,128)(2,1)}), bf16[512,1024]{1,0:T(8,128)(2,1)}) %all-gather.5.cloned.1.call-update) | async-done | bytes 1048592 | tf_op jit(solution)/shard_map/all_gather | solution.py:155
  278.8 1.7 convolution_convert_fusion.1
  281.2 6.6 %fusion.88 = f32[8192,128]{0,1:T(8,128)} fusion(bf16[512,8192]{1,0:T(8,128)(2,1)} %fusion, bf16[512,256]{1,0:T(8,128)(2,1)S(1)} %bitcast.34), kind=kOutput, calls=%fused_computation.156 | convolution fusion | flops 1073741824 | bytes 12713984 | tf_op jit(solution)/shard_map/dot_general | solution.py:54
  287.8 6.6 %fusion.85 = f32[8192,128]{0,1:T(8,128)} fusion(bf16[512,8192]{1,0:T(8,128)(2,1)} %fusion.1, bf16[512,256]{1,0:T(8,128)(2,1)S(1)} %bitcast.35), kind=kOutput, calls=%fused_computation.153 | convolution fusion | flops 1073741824 | bytes 12713984 | tf_op jit(solution)/shard_map/dot_general | solution.py:54
  294.8 8.7 %multiply_convert_fusion = bf16[512,8192]{1,0:T(8,128)(2,1)S(1)} fusion(f32[512,8192]{1,0:T(8,128)} %get-tuple-element.42, f32[512]{0:T(512)S(1)} %multiply_reduce_fusion, f32[512]{0:T(512)S(1)} %log_add_fusion, bf16[8192,256]{1,0:T(8,128)(2,1)} %all-gather.3.cloned.1.call-done, bf16[512,256]{1,0:T(8,128)(2,1)S(1)} %bitcast.37), kind=kOutput, calls=%fused_computation.3 | convolution fusion | flops 1094713344 | bytes 27398144 | tf_op jit(solution)/shard_map/dot_general | solution.py:174
  303.5 3.4 fusion.54
  306.8 1.8 copy-done.5
  308.7 10.4 %multiply_convert_fusion.1 = bf16[512,8192]{1,0:T(8,128)(2,1)} fusion(f32[512,8192]{1,0:T(8,128)} %get-tuple-element.44, f32[512]{0:T(512)S(1)} %multiply_reduce_fusion.1, f32[512]{0:T(512)S(1)} %log_add_fusion.1, bf16[8192,256]{1,0:T(8,128)(2,1)S(1)} %copy-done.5, bf16[512,256]{1,0:T(8,128)(2,1)S(1)} %bitcast.38), kind=kOutput, calls=%fused_computation.4 | convolution fusion | flops 1094713344 | bytes 27398144 | tf_op jit(solution)/shard_map/dot_general | solution.py:174
  319.1 6.9 %fusion.57 = f32[8192,128]{0,1:T(8,128)} fusion(bf16[512,8192]{1,0:T(8,128)(2,1)} %multiply_convert_fusion.1, bf16[512,256]{0,1:T(8,128)(2,1)S(1)} %bitcast.45), kind=kOutput, calls=%fused_computation.96 | convolution fusion | flops 1073741824 | bytes 12713984 | tf_op jit(solution)/shard_map/dot_general | solution.py:54
  326.1 1.6 copy-done.8
  327.7 8.2 %pad_maximum_fusion = f32[8192,512]{0,1:T(8,128)} fusion(f32[8192,128]{0,1:T(8,128)S(1)} %copy-done.7, f32[8192,128]{0,1:T(8,128)S(1)} %copy-done.6, f32[8192,128]{0,1:T(8,128)S(1)} %copy-done.8, f32[8192,128]{0,1:T(8,128)} %fusion.57), kind=kLoop, calls=%fused_computation.2 | loop fusion | flops 12582912 | bytes 33554432 | tf_op jit(solution)/shard_map/concatenate | solution.py:199
  337.2 6.9 %fusion.6 = f32[512,128]{0,1:T(8,128)S(1)} fusion(bf16[512,8192]{1,0:T(8,128)(2,1)} %copy-done.3, bf16[8192,256]{1,0:T(8,128)(2,1)} %bitcast.2), kind=kOutput, calls=%fused_computation.18 | convolution fusion | flops 1073741824 | bytes 10747904 | tf_op jit(solution)/shard_map/dot_general | solution.py:183
  344.1 7.6 %fusion.12 = f32[512,128]{0,1:T(8,128)S(1)} fusion(bf16[512,8192]{1,0:T(8,128)(2,1)} %multiply_convert_fusion.1, bf16[8192,256]{1,0:T(8,128)(2,1)} %bitcast.2), kind=kOutput, calls=%fused_computation.24 | convolution fusion | flops 1073741824 | bytes 10747904 | tf_op jit(solution)/shard_map/dot_general | solution.py:183
  352.9 177.4 %reduce-scatter.5.cloned.1.call-done = f32[1024,512]{0,1:T(8,128)} async-done(((f32[8192,512]{0,1:T(8,128)}), f32[1024,512]{0,1:T(8,128)}) %reduce-scatter.5.cloned.1.call-update) | async-done | bytes 2097168 | tf_op jit(solution)/shard_map/reduce_scatter | solution.py:198
  530.2 1.7 fusion.92
  (100 shorter events, 21.8 us)
Async XLA Ops:
  7.2 144.2 %copy-start = (bf16[256,1024]{1,0:T(8,128)(2,1)S(1)}, bf16[256,1024]{1,0:T(8,128)(2,1)}, u32[]{:S(2)}) copy-start(bf16[256,1024]{1,0:T(8,128)(2,1)} %param.18) | copy-start | bytes 1572868
  9.7 11.3 %copy-start.14 = (s32[32]{0:T(128)S(1)}, s32[32]{0:T(128)}, u32[]{:S(2)}) copy-start(s32[32]{0:T(128)} %param.15) | copy-start | bytes 388
  9.7 11.5 %copy-start.12 = (s32[512]{0:T(512)S(1)}, s32[512]{0:T(512)}, u32[]{:S(2)}) copy-start(s32[512]{0:T(512)} %param.16) | copy-start | bytes 6148
  9.7 11.8 %copy-start.10 = (bf16[512,256]{1,0:T(8,128)(2,1)S(1)}, bf16[512,256]{1,0:T(8,128)(2,1)}, u32[]{:S(2)}) copy-start(bf16[512,256]{1,0:T(8,128)(2,1)} %param.12) | copy-start | bytes 786436
  9.7 11.9 %copy-start.13 = (s32[32]{0:T(128)S(1)}, s32[32]{0:T(128)}, u32[]{:S(2)}) copy-start(s32[32]{0:T(128)} %param.17) | copy-start | bytes 388
  12.2 74.0 %all-to-all-start = ((bf16[8,1024,256]{2,1,0:T(8,128)(2,1)}), bf16[8,1024,256]{2,1,0:T(8,128)(2,1)}, u32[]{:S(2)}, u32[]{:S(2)}) async-start(bf16[8,1024,256]{2,1,0:T(8,128)(2,1)} %stack.2), calls=%async_computation | async-start | bytes 8388608 | tf_op jit(solution)/shard_map/all_to_all | solution.py:17
  19.9 119.1 %all-gather.3.cloned.1.call-start = ((), (), s32[]{:S(2)}) async-start(), calls=%async_computation.3 | async-start | bytes 4718592 | tf_op jit(solution)/shard_map/all_gather | solution.py:102
  20.6 194.5 %reduce-scatter.3.cloned.1.call-start = ((), (), s32[]{:S(2)}) async-start(), calls=%async_computation.4 | async-start | bytes 2228224 | tf_op jit(solution)/shard_map/reduce_scatter | solution.py:142
  120.2 13.7 %copy-start.2 = (f32[512,8192]{1,0:T(8,128)S(1)}, f32[512,8192]{1,0:T(8,128)}, u32[]{:S(2)}) copy-start(f32[512,8192]{1,0:T(8,128)} %get-tuple-element.44) | copy-start | bytes 50331652
  139.0 7.0 %copy-start.4 = (bf16[512,8192]{1,0:T(8,128)(2,1)S(1)}, bf16[512,8192]{1,0:T(8,128)(2,1)}, u32[]{:S(2)}) copy-start(bf16[512,8192]{1,0:T(8,128)(2,1)} %fusion) | copy-start | bytes 25165828
  153.2 125.6 %all-gather.5.cloned.1.call-start = ((), (), s32[]{:S(2)}) async-start(), calls=%async_computation.5 | async-start | bytes 1114112 | tf_op jit(solution)/shard_map/all_gather | solution.py:155
  222.3 8.9 %copy-start.11 = (f32[1024]{0:T(1024)S(1)}, f32[1024]{0:T(1024)}, u32[]{:S(2)}) copy-start(f32[1024]{0:T(1024)} %param.21) | copy-start | bytes 12292
  222.3 13.4 %copy-start.9 = (f32[32,1024]{1,0:T(8,128)S(1)}, f32[32,1024]{1,0:T(8,128)}, u32[]{:S(2)}) copy-start(f32[32,1024]{1,0:T(8,128)} %reduce-scatter.3.cloned.1.call-done) | copy-start | bytes 393220
  247.8 282.4 %reduce-scatter.5.cloned.1.call-start = ((), (), s32[]{:S(2)}) async-start(), calls=%async_computation.6 | async-start | bytes 18874368 | tf_op jit(solution)/shard_map/reduce_scatter | solution.py:198
  303.4 15.7 %copy-start.3 = (bf16[512,8192]{1,0:T(8,128)(2,1)}, bf16[512,8192]{1,0:T(8,128)(2,1)S(1)}, u32[]{:S(2)}) copy-start(bf16[512,8192]{1,0:T(8,128)(2,1)S(1)} %multiply_convert_fusion) | copy-start | bytes 25165828
  303.5 5.2 copy-start.5
  319.1 7.0 %copy-start.6 = (f32[8192,128]{0,1:T(8,128)S(1)}, f32[8192,128]{0,1:T(8,128)}, u32[]{:S(2)}) copy-start(f32[8192,128]{0,1:T(8,128)} %fusion.88) | copy-start | bytes 12582916
  319.1 7.0 %copy-start.7 = (f32[8192,128]{0,1:T(8,128)S(1)}, f32[8192,128]{0,1:T(8,128)}, u32[]{:S(2)}) copy-start(f32[8192,128]{0,1:T(8,128)} %fusion.85) | copy-start | bytes 12582916
  319.1 8.6 %copy-start.8 = (f32[8192,128]{0,1:T(8,128)S(1)}, f32[8192,128]{0,1:T(8,128)}, u32[]{:S(2)}) copy-start(f32[8192,128]{0,1:T(8,128)} %fusion.54) | copy-start | bytes 12582916
  351.7 183.2 %copy-start.1 = (bf16[256,1024]{1,0:T(8,128)(2,1)S(1)}, bf16[256,1024]{1,0:T(8,128)(2,1)}, u32[]{:S(2)}) copy-start(bf16[256,1024]{1,0:T(8,128)(2,1)} %param.18) | copy-start | bytes 1572868
Sparse Core Ops, SparseCore 0:
  23.1 106.2 all-gather.2
  153.3 61.7 reduce-scatter.2
  247.9 30.8 all-gather.4
  336.0 194.1 reduce-scatter.4
